TPU v7x, 32 devices: a whole 2x2x4 slice. The times are simulated.
32 devices in a mesh: dp: 4 (over y, core), tensor: 8 (over z, x).
Axes of the slice: x: 2, y: 2, z: 4, core: 2. Of those that a mesh axis runs over, the one named last changes fastest.
Arguments:
- mixer_input: bfloat16 [256, 8192], P('dp', 'tensor'), may hold values from -6 to 6
- gate_input: bfloat16 [256, 8192], P('dp', 'tensor'), may hold values from -6 to 6
- conv_state: bfloat16 [256, 3, 8192], P('dp', None, 'tensor'), may hold values from -6 to 6
- conv_weight: float32 [4, 8192], P(None, 'tensor'), may hold values from -3 to 3
- conv_bias: float32 [8192], P('tensor'), may hold values from -0.5 to 0.5
- state_proj: bfloat16 [8192, 288], P('tensor'), may hold values from -0.0625 to 0.0625
- step_proj: bfloat16 [256, 8192], P(None, 'tensor'), may hold values from -0.375 to 0.375
- step_bias: float32 [8192], P('tensor'), may hold values from -3 to 0
- decay_rate: float32 [16, 8192], P(None, 'tensor'), may hold values from 0.5 to 16
- skip_gain: float32 [8192], P('tensor'), may hold values from 0.5 to 1.5
- scan_state: float32 [256, 16, 8192], P('dp', None, 'tensor'), may hold values from -6 to 6
- output_proj: bfloat16 [8192, 4096], P('tensor'), may hold values from -0.09375 to 0.09375
- residual: bfloat16 [256, 4096], P('dp', 'tensor'), may hold values from -6 to 6
- router: bfloat16 [4096, 4], replicated, may hold values from -0.09375 to 0.09375
- expert_ids: int32 [256, 2], P('dp'), may hold values from 0 to 3, all different within a row; in each aligned block of 64 rows (0 to 63, 64 to 127, ...) at most 40 rows name the same one
- active: int32 [256], P('dp'), may hold values 0 or 1
- up_weight: bfloat16 [4, 4096, 14336], P('dp', None, 'tensor'), may hold values from -0.09375 to 0.09375
- down_weight: bfloat16 [4, 14336, 4096], P('dp', 'tensor'), may hold values from -0.0625 to 0.0625
Outputs:
- layer_out: bfloat16 [256, 4096], P('dp', 'tensor')
- state_out: float32 [256, 16, 8192], P('dp', None, 'tensor')
- conv_cache: bfloat16 [256, 3, 8192], P('dp', None, 'tensor')
Inputs may be any that keep to these rules, and one draw needn't show every extreme that they name: `expert_ids`: each row names two different experts; within each aligned block of 64 sessions (the sessions of one index of dp) no expert is named by more than 40 rows, a bound that some block reaches.
All inputs are finite; a program needn't handle non-finite values. No bound on the sum of `active` on one device may be relied on, other than what follows from the above.
Results may differ from a plain program's by a relative error of at most 0.02.
Values may be sent and summed in bfloat16 or wider, within the bound.
A program may use at most 128 MiB of HBM per device.

v0:
```python
import jax
import jax.numpy as jnp
from jax import lax
from jax.sharding import PartitionSpec as P

DM = 4096
CAP = 40


def local(
    mixer_input,
    gate_input,
    conv_state,
    conv_weight,
    conv_bias,
    state_proj,
    step_proj,
    step_bias,
    decay_rate,
    skip_gain,
    scan_state,
    output_proj,
    residual,
    router,
    expert_ids,
    active,
    up_weight,
    down_weight,
):
    window = jnp.concatenate([conv_state, mixer_input[:, None, :]], axis=1)
    conv_sum = jnp.sum(window.astype(jnp.float32) * conv_weight[None], axis=1) + conv_bias
    conv_out = jax.nn.silu(conv_sum).astype(jnp.bfloat16)
    partial_proj = jnp.dot(conv_out, state_proj, preferred_element_type=jnp.float32)
    projected = lax.psum(partial_proj.astype(jnp.bfloat16), "tensor").astype(jnp.float32)
    low_rank = step_proj.shape[0]
    states = decay_rate.shape[0]
    step_raw = projected[:, :low_rank]
    input_map = projected[:, low_rank : low_rank + states]
    output_map = projected[:, low_rank + states :]
    step_norm = (
        step_raw * lax.rsqrt(jnp.mean(step_raw * step_raw, axis=1, keepdims=True) + 1e-06)
    ).astype(jnp.bfloat16)
    step_size = jax.nn.softplus(
        jnp.dot(step_norm, step_proj, preferred_element_type=jnp.float32) + step_bias
    )
    conv_float = conv_out.astype(jnp.float32)
    state_next = (
        jnp.exp(-step_size[:, None, :] * decay_rate[None]) * scan_state
        + (step_size * conv_float)[:, None, :] * input_map[:, :, None]
    )
    live_float = active.astype(jnp.float32)
    live_mask = active == 1
    scan_out = jnp.sum(output_map[:, :, None] * state_next, axis=1) + skip_gain * conv_float
    gated = (scan_out * jax.nn.silu(gate_input.astype(jnp.float32)) * live_float[:, None]).astype(
        jnp.bfloat16
    )
    state_out = jnp.where(live_mask[:, None, None], state_next, scan_state)
    conv_cache = jnp.where(live_mask[:, None, None], window[:, 1:, :], conv_state)
    experts_total = router.shape[1]
    sessions = expert_ids.shape[0]
    flat_ids = expert_ids.reshape(-1)
    one_hot = (flat_ids[:, None] == jnp.arange(experts_total, dtype=jnp.int32)[None, :]).astype(
        jnp.int32
    )
    slot_index = jnp.sum((jnp.cumsum(one_hot, axis=0) - one_hot) * one_hot, axis=1).reshape(
        sessions, 2
    )
    buffer_row = expert_ids * CAP + slot_index
    row_numbers = jnp.arange(experts_total * CAP, dtype=jnp.int32)
    placement = jnp.sum(
        ((buffer_row[None] == row_numbers[:, None, None]) & live_mask[None, :, None]).astype(
            jnp.float32
        ),
        axis=2,
    ).astype(jnp.bfloat16)
    slice_width = residual.shape[1]
    offset = lax.axis_index("tensor") * slice_width
    up_rows = up_weight[0]
    mixer_part = jnp.dot(gated, output_proj, preferred_element_type=jnp.float32)
    own_cols = lax.dynamic_slice_in_dim(mixer_part, offset, slice_width, 1) + residual.astype(
        jnp.float32
    )
    mixer_part = lax.dynamic_update_slice_in_dim(mixer_part, own_cols, offset, 1)
    hidden_sum = lax.psum(mixer_part.astype(jnp.bfloat16), "tensor").astype(jnp.float32)
    square_sum = jnp.sum(hidden_sum * hidden_sum, axis=1)
    raw_logits = jnp.dot(hidden_sum, router.astype(jnp.float32), precision=lax.Precision.HIGHEST)
    inv_rms = lax.rsqrt(square_sum / DM + 1e-06)
    hidden_local = lax.dynamic_slice_in_dim(hidden_sum, offset, slice_width, 1)
    normed = (hidden_sum * inv_rms[:, None]).astype(jnp.bfloat16)
    outgoing = jnp.dot(placement, normed, preferred_element_type=jnp.float32).astype(jnp.bfloat16)
    outgoing = outgoing.reshape(experts_total, CAP, normed.shape[1])
    incoming = lax.all_to_all(outgoing, "dp", split_axis=0, concat_axis=0, tiled=True)
    up_sum = jnp.dot(
        incoming.reshape(-1, incoming.shape[2]), up_rows, preferred_element_type=jnp.float32
    )
    hidden = jax.nn.silu(up_sum).astype(jnp.bfloat16)
    down_rows = down_weight[0]
    expert_share = lax.psum_scatter(
        lax.dot_general(
            down_rows, hidden, (((0,), (1,)), ((), ())), preferred_element_type=jnp.float32
        ).astype(jnp.bfloat16),
        "tensor",
        scatter_dimension=0,
        tiled=True,
    ).astype(jnp.float32)
    replies = expert_share.T.astype(jnp.bfloat16).reshape(-1, CAP, slice_width)
    returned = lax.all_to_all(replies, "dp", split_axis=0, concat_axis=0, tiled=True)
    gathered = returned.reshape(-1, slice_width)[buffer_row]
    chosen_logit = jnp.take_along_axis(raw_logits, expert_ids, axis=1) * inv_rms[:, None]
    first = 1.0 / (1.0 + jnp.exp(chosen_logit[:, 1] - chosen_logit[:, 0]))
    second = 1.0 / (1.0 + jnp.exp(chosen_logit[:, 0] - chosen_logit[:, 1]))
    route_weight = jnp.stack([first, second], axis=1) * live_float[:, None]
    layer_out = (
        hidden_local + jnp.sum(route_weight[:, :, None] * gathered.astype(jnp.float32), axis=1)
    ).astype(jnp.bfloat16)
    return (layer_out, state_out, conv_cache)


def solution(mesh):
    placed = (
        P("dp", "tensor"),
        P("dp", "tensor"),
        P("dp", None, "tensor"),
        P(None, "tensor"),
        P("tensor"),
        P("tensor", None),
        P(None, "tensor"),
        P("tensor"),
        P(None, "tensor"),
        P("tensor"),
        P("dp", None, "tensor"),
        P("tensor", None),
        P("dp", "tensor"),
        P(),
        P("dp", None),
        P("dp"),
        P("dp", None, "tensor"),
        P("dp", "tensor", None),
    )
    return jax.shard_map(
        local,
        mesh=mesh,
        in_specs=placed,
        out_specs=(P("dp", "tensor"), P("dp", None, "tensor"), P("dp", None, "tensor")),
        check_vma=False,
    )
```

profile of v0, /device:TPU:11, one launch (start us, length us, event | category | flops | bytes accessed | tf_op | source)
XLA Modules:
  0.0 248.5 jit_solution(16056825257584524228)
XLA Ops:
  7.2 0.0 copy-start
  7.2 0.0 copy-start.6
  7.2 0.0 all-reduce.2.cloned.1.call-start
  7.2 1.2 multiply_reduce_fusion.2
  8.4 0.0 copy-done
  8.5 1.0 convolution_convert_fusion.1
  9.5 23.7 %psum.14 = bf16[64,288]{1,0:T(8,128)(2,1)S(1)} all-reduce(bf16[64,288]{1,0:T(8,128)(2,1)S(1)} %convolution_convert_fusion.1), channel_id=1, replica_groups=mesh['dp'=4,'tensor'=8] {'tensor'}, use_global_device_ids=true, to_apply=%region_1.2 | all-reduce | flops 18432 | bytes 73728 | tf_op jit(solution)/shard_map/psum | solution.py:34
  33.2 0.1 fusion.40
  33.3 0.7 broadcast_compare_fusion
  34.0 0.7 convert_element_type.79
  34.6 0.1 multiply_reduce_fusion.4
  34.8 1.5 fusion.39
  36.2 0.0 copy-done.6
  36.2 0.0 copy-start.1
  36.3 0.0 copy-start.5
  36.3 0.0 copy-start.8
  36.3 0.0 copy-start.9
  36.3 5.2 %fusion.10 = (f32[64,16,1024]{2,1,0:T(8,128)}, f32[64,1024]{1,0:T(8,128)S(1)}) fusion(f32[64,16,1024]{2,1,0:T(8,128)} %param.28, f32[64,16]{1,0:T(8,128)S(1)} %get-tuple-element.10, f32[64,1024]{1,0:T(8,128)S(1)} %get-tuple-element.8, f32[16,1024]{1,0:T(8,128)S(1)} %copy-done.6, f32[64,1024]{1,0:T(8,128)S(1)} %get-tuple-element.7, ...), kind=kLoop, calls=%fused_computation.11 | loop fusion | flops 7274496 | bytes 9248832 | tf_op jit(solution)/shard_map/jit(_where)/select_n | solution.py:57
  41.5 0.9 copy-done.1
  42.4 0.0 copy-done.5
  42.4 0.0 copy-done.8
  42.4 0.0 copy-done.9
  42.4 0.0 copy-start.11
  42.4 1.7 fusion.27
  44.1 0.0 copy-done.7
  44.2 0.8 convert_element_type.82
  45.0 0.0 all-reduce.2.cloned.1.call-update
  45.1 0.0 reduce-scatter.2.cloned.1.call-start
  45.1 0.0 copy-done.11
  45.1 0.1 copy.71
  45.2 0.1 eq.34
  45.4 0.1 fusion.33
  45.4 0.2 reduce_window_sum.11
  45.6 0.2 select_reduce_fusion
  45.8 0.1 reshape.87
  45.9 0.1 copy.72
  46.0 0.1 convert_reduce_fusion
  46.1 80.9 %all-reduce.2.cloned.1.call-done = bf16[64,4096]{1,0:T(8,128)(2,1)} async-done(((bf16[64,4096]{1,0:T(8,128)(2,1)}), bf16[64,4096]{1,0:T(8,128)(2,1)}) %all-reduce.2.cloned.1.call-update) | async-done | bytes 524304 | tf_op jit(solution)/shard_map/psum | solution.py:84
  127.1 1.2 multiply_reduce_fusion.1
  128.3 1.6 convolution_convert_fusion
  129.9 20.9 %all_to_all.10 = bf16[4,40,4096]{2,1,0:T(8,128)(2,1)S(1)} all-to-all(bf16[4,40,4096]{2,1,0:T(8,128)(2,1)S(1)} %bitcast.35), channel_id=1, replica_groups=mesh['dp'=4,'tensor'=8] {'dp'}, dimensions={0} | all-to-all | bytes 2621440 | tf_op jit(solution)/shard_map/all_to_all | solution.py:92
  150.8 15.9 %fusion.7 = bf16[4096,160]{0,1:T(8,128)(2,1)} fusion(bf16[1,1792,4096]{2,1,0:T(8,128)(2,1)} %param.35, bf16[160,4096]{1,0:T(8,128)(2,1)S(1)} %bitcast.36, bf16[1,4096,1792]{2,1,0:T(8,128)(2,1)} %param.34), kind=kOutput, calls=%fused_computation.8 | convolution fusion | flops 4699709440 | bytes 31981568 | tf_op jit(solution)/shard_map/dot_general | solution.py:99
  166.7 0.0 reduce-scatter.2.cloned.1.call-update
  166.7 0.1 copy.73
  166.8 0.1 reshape.94
  167.0 0.1 copy.68
  167.1 0.1 reshape.100
  167.2 0.0 copy-done.3
  167.2 0.0 copy-done.4
  167.2 0.9 fusion.19
  168.1 0.0 copy-done.2
  168.1 0.2 fusion.41
  168.3 1.5 gather_fusion.1
  169.9 0.1 reshape.103
  170.0 0.1 copy.69
  170.1 59.6 %reduce-scatter.2.cloned.1.call-done = bf16[512,160]{0,1:T(8,128)(2,1)} async-done(((bf16[4096,160]{0,1:T(8,128)(2,1)}), bf16[512,160]{0,1:T(8,128)(2,1)}) %reduce-scatter.2.cloned.1.call-update) | async-done | bytes 163856 | tf_op jit(solution)/shard_map/reduce_scatter | solution.py:98
  229.7 6.0 %all-to-all-start.1 = ((bf16[4,40,512]{2,1,0:T(8,128)(2,1)}), bf16[4,40,512]{2,1,0:T(8,128)(2,1)S(1)}, u32[]{:S(2)}, u32[]{:S(2)}) async-start(bf16[4,40,512]{2,1,0:T(8,128)(2,1)} %bitcast.39), calls=%async_computation.2 | async-start | bytes 327680 | tf_op jit(solution)/shard_map/all_to_all | solution.py:107
  235.7 0.1 copy.70
  235.8 0.1 convert_element_type.83
  235.9 3.6 %all-to-all-done.1 = bf16[4,40,512]{2,1,0:T(8,128)(2,1)S(1)} async-done(((bf16[4,40,512]{2,1,0:T(8,128)(2,1)}), bf16[4,40,512]{2,1,0:T(8,128)(2,1)S(1)}, u32[]{:S(2)}, u32[]{:S(2)}) %all-to-all-start.1) | async-done | bytes 163872 | tf_op jit(solution)/shard_map/all_to_all | solution.py:107
  239.5 0.8 gather_fusion
  240.4 0.2 reshape.108
  240.6 0.4 multiply_reduce_fusion.3
  241.0 0.7 add_convert_fusion
  (16 shorter events, 0.1 us)
Async XLA Ops:
  7.2 1.3 copy-start
  7.2 29.1 %copy-start.6 = (f32[16,1024]{1,0:T(8,128)S(1)}, f32[16,1024]{1,0:T(8,128)}, u32[]{:S(2)}) copy-start(f32[16,1024]{1,0:T(8,128)} %param.26) | copy-start | bytes 196612
  7.2 119.9 %all-reduce.2.cloned.1.call-start = ((), (), s32[]{:S(2)}) async-start(), calls=%async_computation.3 | async-start | bytes 1048576 | tf_op jit(solution)/shard_map/psum | solution.py:84
  36.2 6.2 %copy-start.1 = (bf16[1024,4096]{1,0:T(8,128)(2,1)S(1)}, bf16[1024,4096]{1,0:T(8,128)(2,1)}, u32[]{:S(2)}) copy-start(bf16[1024,4096]{1,0:T(8,128)(2,1)} %param.29) | copy-start | bytes 25165828
  36.3 6.2 %copy-start.5 = (bf16[64,1024]{1,0:T(8,128)(2,1)S(1)}, bf16[64,1024]{1,0:T(8,128)(2,1)}, u32[]{:S(2)}) copy-start(bf16[64,1024]{1,0:T(8,128)(2,1)} %param.19) | copy-start | bytes 393220
  36.3 6.1 %copy-start.8 = (f32[1024]{0:T(1024)S(1)}, f32[1024]{0:T(1024)}, u32[]{:S(2)}) copy-start(f32[1024]{0:T(1024)} %param.22) | copy-start | bytes 12292
  36.3 6.1 %copy-start.9 = (f32[1024]{0:T(1024)S(1)}, f32[1024]{0:T(1024)}, u32[]{:S(2)}) copy-start(f32[1024]{0:T(1024)} %param.27) | copy-start | bytes 12292
  42.4 1.7 copy-start.7
  42.4 2.7 %copy-start.11 = (s32[64,2]{0,1:T(2,128)S(1)}, s32[64,2]{0,1:T(2,128)}, u32[]{:S(2)}) copy-start(s32[64,2]{0,1:T(2,128)} %param.32) | copy-start | bytes 1540
  45.1 184.6 %reduce-scatter.2.cloned.1.call-start = ((), (), s32[]{:S(2)}) async-start(), calls=%async_computation.4 | async-start | bytes 1474560 | tf_op jit(solution)/shard_map/reduce_scatter | solution.py:98
  150.8 16.4 %copy-start.3 = (bf16[64,3,1024]{2,0,1:T(8,128)(2,1)S(1)}, bf16[64,3,1024]{2,0,1:T(8,128)(2,1)}, u32[]{:S(2)}) copy-start(bf16[64,3,1024]{2,0,1:T(8,128)(2,1)} %param.20) | copy-start | bytes 1179652
  150.8 16.4 %copy-start.4 = (bf16[64,1024]{1,0:T(8,128)(2,1)S(1)}, bf16[64,1024]{1,0:T(8,128)(2,1)}, u32[]{:S(2)}) copy-start(bf16[64,1024]{1,0:T(8,128)(2,1)} %param.18) | copy-start | bytes 393220
  150.8 17.3 %copy-start.2 = (bf16[64,4096]{1,0:T(8,128)(2,1)S(1)}, bf16[64,4096]{1,0:T(8,128)(2,1)}, u32[]{:S(2)}) copy-start(bf16[64,4096]{1,0:T(8,128)(2,1)} %all-reduce.2.cloned.1.call-done) | copy-start | bytes 1572868
  150.8 17.3 %copy-start.10 = (bf16[4096,4]{0,1:T(4,128)(2,1)S(1)}, bf16[4096,4]{0,1:T(4,128)(2,1)}, u32[]{:S(2)}) copy-start(bf16[4096,4]{0,1:T(4,128)(2,1)} %param.31) | copy-start | bytes 98308
  229.7 9.9 %all-to-all-start.1 = ((bf16[4,40,512]{2,1,0:T(8,128)(2,1)}), bf16[4,40,512]{2,1,0:T(8,128)(2,1)S(1)}, u32[]{:S(2)}, u32[]{:S(2)}) async-start(bf16[4,40,512]{2,1,0:T(8,128)(2,1)} %bitcast.39), calls=%async_computation.2 | async-start | bytes 327680 | tf_op jit(solution)/shard_map/all_to_all | solution.py:107
Sparse Core Ops, SparseCore 0:
  45.2 81.8 all-reduce.1
  166.8 62.8 reduce-scatter.1
where the time goes:
time: 251 us; the launch traced here: 248 us
  waiting for transfers between devices  144 us (57%)
  blocking collectives  44.6 us (18%)
  matrix products  21.9 us (9%)
  between operations  14.3 us (6%)
  other arithmetic  12.6 us (5%)
  starting transfers between devices  6.1 us (2%)
  local copies, waits for them, and re-layouts  4.78 us (2%)
    psum x1, waiting for transfers between devices, local(): lax.psum(mixer_part.astype(jnp.bfloat16), 'tensor').astype(jnp.float32)  80.9 us
    reduce_scatter x1, waiting for transfers between devices, local(): lax.psum_scatter(lax.dot_general(down_rows, hidden, (((0,), (1,)), ((), (...  59.6 us
    psum x1, blocking collectives, local(): lax.psum(partial_proj.astype(jnp.bfloat16), 'tensor').astype(jnp.float32)  23.7 us
    all_to_all x1, blocking collectives, local(): lax.all_to_all(outgoing, 'dp', split_axis=0, concat_axis=0, tiled=True)  20.9 us
    dot_general x1, matrix products, local(): lax.dot_general(down_rows, hidden, (((0,), (1,)), ((), ())), preferred_el...  15.9 us
    all_to_all x1, starting transfers between devices, local(): lax.all_to_all(replies, 'dp', split_axis=0, concat_axis=0, tiled=True)  6.02 us
    select_n x1, other arithmetic, local(): state_out = jnp.where(live_mask[:, None, None], state_next, scan_state)  5.23 us
  transfers between devices with their start and end apart: 3, of which 3 were waited for; matrix products, arithmetic and copies ran while one was open for 2% of the time, Pallas kernels for 0%

commit v1 on v0

--- a/solution.py
+++ b/solution.py
@@ -1,13 +1,232 @@
+import functools
+
 import jax
 import jax.numpy as jnp
 from jax import lax
+from jax.experimental import pallas as pl
+from jax.experimental.pallas import tpu as pltpu
 from jax.sharding import PartitionSpec as P
 
 DM = 4096
 CAP = 40
 
 
+VMEM = pl.BlockSpec(memory_space=pltpu.VMEM)
+
+
+def greet(groups):
+    barrier = pltpu.get_barrier_semaphore()
+    for axis, size in groups:
+        me = lax.axis_index(axis)
+        for k in range(1, size):
+            pl.semaphore_signal(
+                barrier,
+                inc=1,
+                device_id={axis: lax.rem(me + k, size)},
+                device_id_type=pl.DeviceIdType.MESH,
+            )
+    pl.semaphore_wait(barrier, sum(size - 1 for _, size in groups))
+
+
+def send_all(axis, size, source, target, send_sem, recv_sem):
+    me = lax.axis_index(axis)
+    copies = []
+    for k in range(1, size):
+        peer = lax.rem(me + k, size)
+        copy = pltpu.make_async_remote_copy(
+            src_ref=source(peer, k),
+            dst_ref=target(me, k),
+            send_sem=send_sem.at[k - 1],
+            recv_sem=recv_sem.at[k - 1],
+            device_id={axis: peer},
+            device_id_type=pl.DeviceIdType.MESH,
+        )
+        copy.start()
+        copies.append(copy)
+    return copies
+
+
+def columns(ref, index, width):
+    return ref.at[:, pl.ds(pl.multiple_of(index * width, width), width)]
+
+
+def sum_rows_kernel(size, x_ref, out_ref, landed, send_a, recv_a, send_b, recv_b):
+    me = lax.axis_index("tensor")
+    greet((("tensor", size),))
+    copies = send_all(
+        "tensor",
+        size,
+        lambda peer, k: x_ref.at[peer],
+        lambda mine, k: landed.at[k - 1],
+        send_a,
+        recv_a,
+    )
+    total = x_ref[me]
+    for k, copy in enumerate(copies):
+        copy.wait_recv()
+        total += landed[k]
+    out_ref[me] = total
+    back = send_all(
+        "tensor",
+        size,
+        lambda peer, k: out_ref.at[me],
+        lambda mine, k: out_ref.at[mine],
+        send_b,
+        recv_b,
+    )
+    for copy in copies:
+        copy.wait_send()
+    for copy in back:
+        copy.wait()
+
+
+def sum_rows(x, size, collective_id):
+    rows, width = x.shape
+    chunks = x.reshape(size, rows // size, width)
+    out = pl.pallas_call(
+        functools.partial(sum_rows_kernel, size),
+        out_shape=jax.ShapeDtypeStruct(chunks.shape, x.dtype),
+        in_specs=[VMEM],
+        out_specs=VMEM,
+        scratch_shapes=[pltpu.VMEM((size - 1,) + chunks.shape[1:], x.dtype)]
+        + [pltpu.SemaphoreType.DMA((size - 1,))] * 4,
+        compiler_params=pltpu.CompilerParams(collective_id=collective_id, has_side_effects=True),
+    )(chunks)
+    return out.reshape(rows, width)
+
+
+def sum_columns_kernel(size, x_ref, add_ref, out_ref, landed, total, send_a, recv_a, send_b, recv_b):
+    me = lax.axis_index("tensor")
+    width = add_ref.shape[1]
+    greet((("tensor", size),))
+    copies = send_all(
+        "tensor",
+        size,
+        lambda peer, k: columns(x_ref, peer, width),
+        lambda mine, k: landed.at[k - 1],
+        send_a,
+        recv_a,
+    )
+    total[...] = add_ref[...].astype(jnp.float32) + columns(x_ref, me, width)[...].astype(jnp.float32)
+    for k, copy in enumerate(copies):
+        copy.wait_recv()
+        total[...] += landed[k].astype(jnp.float32)
+    columns(out_ref, me, width)[...] = total[...].astype(out_ref.dtype)
+    back = send_all(
+        "tensor",
+        size,
+        lambda peer, k: columns(out_ref, me, width),
+        lambda mine, k: columns(out_ref, mine, width),
+        send_b,
+        recv_b,
+    )
+    for copy in copies:
+        copy.wait_send()
+    for copy in back:
+        copy.wait()
+
+
+def sum_columns(x, add, size, collective_id):
+    rows, width = add.shape
+    return pl.pallas_call(
+        functools.partial(sum_columns_kernel, size),
+        out_shape=jax.ShapeDtypeStruct(x.shape, x.dtype),
+        in_specs=[VMEM] * 2,
+        out_specs=VMEM,
+        scratch_shapes=[
+            pltpu.VMEM((size - 1, rows, width), x.dtype),
+            pltpu.VMEM((rows, width), jnp.float32),
+        ]
+        + [pltpu.SemaphoreType.DMA((size - 1,))] * 4,
+        compiler_params=pltpu.CompilerParams(collective_id=collective_id, has_side_effects=True),
+    )(x, add)
+
+
+def dispatch_kernel(size, x_ref, out_ref, local_sem, send_sem, recv_sem):
+    me = lax.axis_index("dp")
+    greet((("dp", size),))
+    copies = send_all(
+        "dp",
+        size,
+        lambda peer, k: x_ref.at[peer],
+        lambda mine, k: out_ref.at[mine],
+        send_sem,
+        recv_sem,
+    )
+    own = pltpu.make_async_copy(x_ref.at[me], out_ref.at[me], local_sem)
+    own.start()
+    own.wait()
+    for copy in copies:
+        copy.wait()
+
+
+def dispatch(x, size, collective_id):
+    return pl.pallas_call(
+        functools.partial(dispatch_kernel, size),
+        out_shape=jax.ShapeDtypeStruct(x.shape, x.dtype),
+        in_specs=[VMEM],
+        out_specs=VMEM,
+        scratch_shapes=[pltpu.SemaphoreType.DMA] + [pltpu.SemaphoreType.DMA((size - 1,))] * 2,
+        compiler_params=pltpu.CompilerParams(collective_id=collective_id, has_side_effects=True),
+    )(x)
+
+
+def combine_kernel(size, groups, x_ref, out_ref, landed, total, reply, send_a, recv_a, send_b, recv_b):
+    me = lax.axis_index("tensor")
+    home = lax.axis_index("dp")
+    width = total.shape[1]
+    rows = reply.shape[1]
+    greet((("tensor", size), ("dp", groups)))
+    copies = send_all(
+        "tensor",
+        size,
+        lambda peer, k: columns(x_ref, peer, width),
+        lambda mine, k: landed.at[k - 1],
+        send_a,
+        recv_a,
+    )
+    total[...] = columns(x_ref, me, width)[...].astype(jnp.float32)
+    for k, copy in enumerate(copies):
+        copy.wait_recv()
+        total[...] += landed[k].astype(jnp.float32)
+    for block in range(groups):
+        reply[block] = total[block * rows : (block + 1) * rows, :].astype(reply.dtype)
+    back = send_all(
+        "dp",
+        groups,
+        lambda peer, k: reply.at[peer],
+        lambda mine, k: out_ref.at[mine],
+        send_b,
+        recv_b,
+    )
+    out_ref[home] = reply[home]
+    for copy in copies:
+        copy.wait_send()
+    for copy in back:
+        copy.wait()
+
+
+def combine(x, size, groups, collective_id):
+    rows, width = x.shape[0] // groups, x.shape[1] // size
+    return pl.pallas_call(
+        functools.partial(combine_kernel, size, groups),
+        out_shape=jax.ShapeDtypeStruct((groups, rows, width), x.dtype),
+        in_specs=[VMEM],
+        out_specs=VMEM,
+        scratch_shapes=[
+            pltpu.VMEM((size - 1, x.shape[0], width), x.dtype),
+            pltpu.VMEM((x.shape[0], width), jnp.float32),
+            pltpu.VMEM((groups, rows, width), x.dtype),
+        ]
+        + [pltpu.SemaphoreType.DMA((size - 1,))] * 2
+        + [pltpu.SemaphoreType.DMA((groups - 1,))] * 2,
+        compiler_params=pltpu.CompilerParams(collective_id=collective_id, has_side_effects=True),
+    )(x)
+
+
 def local(
+    n_tensor,
+    n_dp,
     mixer_input,
     gate_input,
     conv_state,
@@ -31,7 +250,7 @@
     conv_sum = jnp.sum(window.astype(jnp.float32) * conv_weight[None], axis=1) + conv_bias
     conv_out = jax.nn.silu(conv_sum).astype(jnp.bfloat16)
     partial_proj = jnp.dot(conv_out, state_proj, preferred_element_type=jnp.float32)
-    projected = lax.psum(partial_proj.astype(jnp.bfloat16), "tensor").astype(jnp.float32)
+    projected = sum_rows(partial_proj, n_tensor, 0)
     low_rank = step_proj.shape[0]
     states = decay_rate.shape[0]
     step_raw = projected[:, :low_rank]
@@ -77,11 +296,9 @@
     offset = lax.axis_index("tensor") * slice_width
     up_rows = up_weight[0]
     mixer_part = jnp.dot(gated, output_proj, preferred_element_type=jnp.float32)
-    own_cols = lax.dynamic_slice_in_dim(mixer_part, offset, slice_width, 1) + residual.astype(
+    hidden_sum = sum_columns(mixer_part.astype(jnp.bfloat16), residual, n_tensor, 1).astype(
         jnp.float32
     )
-    mixer_part = lax.dynamic_update_slice_in_dim(mixer_part, own_cols, offset, 1)
-    hidden_sum = lax.psum(mixer_part.astype(jnp.bfloat16), "tensor").astype(jnp.float32)
     square_sum = jnp.sum(hidden_sum * hidden_sum, axis=1)
     raw_logits = jnp.dot(hidden_sum, router.astype(jnp.float32), precision=lax.Precision.HIGHEST)
     inv_rms = lax.rsqrt(square_sum / DM + 1e-06)
@@ -89,22 +306,14 @@
     normed = (hidden_sum * inv_rms[:, None]).astype(jnp.bfloat16)
     outgoing = jnp.dot(placement, normed, preferred_element_type=jnp.float32).astype(jnp.bfloat16)
     outgoing = outgoing.reshape(experts_total, CAP, normed.shape[1])
-    incoming = lax.all_to_all(outgoing, "dp", split_axis=0, concat_axis=0, tiled=True)
+    incoming = dispatch(outgoing, n_dp, 2)
     up_sum = jnp.dot(
         incoming.reshape(-1, incoming.shape[2]), up_rows, preferred_element_type=jnp.float32
     )
     hidden = jax.nn.silu(up_sum).astype(jnp.bfloat16)
     down_rows = down_weight[0]
-    expert_share = lax.psum_scatter(
-        lax.dot_general(
-            down_rows, hidden, (((0,), (1,)), ((), ())), preferred_element_type=jnp.float32
-        ).astype(jnp.bfloat16),
-        "tensor",
-        scatter_dimension=0,
-        tiled=True,
-    ).astype(jnp.float32)
-    replies = expert_share.T.astype(jnp.bfloat16).reshape(-1, CAP, slice_width)
-    returned = lax.all_to_all(replies, "dp", split_axis=0, concat_axis=0, tiled=True)
+    expert_part = jnp.dot(hidden, down_rows, preferred_element_type=jnp.float32)
+    returned = combine(expert_part.astype(jnp.bfloat16), n_tensor, n_dp, 3)
     gathered = returned.reshape(-1, slice_width)[buffer_row]
     chosen_logit = jnp.take_along_axis(raw_logits, expert_ids, axis=1) * inv_rms[:, None]
     first = 1.0 / (1.0 + jnp.exp(chosen_logit[:, 1] - chosen_logit[:, 0]))
@@ -138,7 +347,7 @@
         P("dp", "tensor", None),
     )
     return jax.shard_map(
-        local,
+        functools.partial(local, mesh.shape["tensor"], mesh.shape["dp"]),
         mesh=mesh,
         in_specs=placed,
         out_specs=(P("dp", "tensor"), P("dp", None, "tensor"), P("dp", None, "tensor")),

time: 251 us -> 142 us (0.57)
  waiting for transfers between devices: 144 us -> 0 us
  Pallas kernels: 0 us -> 97.6 us
  blocking collectives: 44.6 us -> 0 us
  between operations: 14.3 us -> 0.96 us
  starting transfers between devices: 6.1 us -> 0 us
  matrix products: 21.9 us -> 24.8 us
    pallas_call x0 -> x4, Pallas kernels: none -> 97.6 us  [the longest x1 37.9 us: combine(): pl.pallas_call(functools.partial(combine_kernel, size, groups), out_shape...]
    psum x1 -> x0, waiting for transfers between devices: 80.9 us -> none  [local(): lax.psum(mixer_part.astype(jnp.bfloat16), 'tensor').astype(jnp.float32)]
    reduce_scatter x1 -> x0, waiting for transfers between devices: 59.6 us -> none  [local(): lax.psum_scatter(lax.dot_general(down_rows, hidden, (((0,), (1,)), ((), (...]
    psum x1 -> x0, blocking collectives: 23.7 us -> none  [local(): lax.psum(partial_proj.astype(jnp.bfloat16), 'tensor').astype(jnp.float32)]
    all_to_all x1 -> x0, blocking collectives: 20.9 us -> none  [local(): lax.all_to_all(outgoing, 'dp', split_axis=0, concat_axis=0, tiled=True)]
    all_to_all x1 -> x0, starting transfers between devices: 6.02 us -> none  [local(): lax.all_to_all(replies, 'dp', split_axis=0, concat_axis=0, tiled=True)]
    all_to_all x1 -> x0, waiting for transfers between devices: 3.65 us -> none  [local(): lax.all_to_all(replies, 'dp', split_axis=0, concat_axis=0, tiled=True)]
  transfers between devices with their start and end apart: 3 -> 0, of which waited for: 3 -> 0; matrix products, arithmetic and copies ran while one was open for 2% -> 0% of each run, Pallas kernels for 0% -> 0%
where the time goes in v1:
time: 142 us; the launch traced here: 141 us
  Pallas kernels  97.6 us (69%)
  matrix products  24.8 us (17%)
  other arithmetic  11.2 us (8%)
  local copies, waits for them, and re-layouts  6.6 us (5%)
    pallas_call x1, Pallas kernels, combine(): pl.pallas_call(functools.partial(combine_kernel, size, groups), out_shape...  37.9 us
    pallas_call x1, Pallas kernels, sum_columns(): pl.pallas_call(functools.partial(sum_columns_kernel, size), out_shape=jax...  27.6 us
    pallas_call x1, Pallas kernels, dispatch(): pl.pallas_call(functools.partial(dispatch_kernel, size), out_shape=jax.Sh...  20.5 us
    dot_general x1, matrix products, local(): expert_part = jnp.dot(hidden, down_rows, preferred_element_type=jnp.float32)  16.2 us
    pallas_call x1, Pallas kernels, sum_rows(): pl.pallas_call(functools.partial(sum_rows_kernel, size), out_shape=jax.Sh...  11.6 us
    select_n x1, other arithmetic, local(): state_out = jnp.where(live_mask[:, None, None], state_next, scan_state)  5.23 us

profile of v1, /device:TPU:11, one launch (start us, length us, event | category | flops | bytes accessed | tf_op | source)
XLA Modules:
  0.0 141.2 jit_solution(13685565778925791358)
XLA Ops:
  0.6 0.0 copy-start
  0.6 0.0 copy-start.6
  0.7 0.0 copy-start.11
  0.7 1.2 multiply_reduce_fusion.2
  1.9 0.0 copy-done
  1.9 1.7 %convolution_bitcast_fusion.x_ref = f32[8,8,288]{2,1,0:T(8,128)} fusion(bf16[1024,288]{0,1:T(8,128)(2,1)S(1)} %copy-done, f32[64,1024]{1,0:T(8,128)S(1)} %multiply_reduce_fusion.2, f32[1024]{0:T(1024)} %param.22), kind=kOutput, calls=%fused_computation.14 | convolution fusion | flops 38141952 | bytes 929792 | tf_op jit(solution)/shard_map/dot_general | solution.py:252
  3.6 11.6 %shard_map.193 = f32[8,8,288]{2,1,0:T(8,128)} custom-call(f32[8,8,288]{2,1,0:T(8,128)} %convolution_bitcast_fusion.x_ref), custom_call_target="tpu_custom_call" | custom-call | tf_op jit(solution)/shard_map/pallas_call | solution.py:86
  15.2 0.9 fusion.36
  16.1 0.9 multiply_reduce_fusion.4
  17.1 1.5 %fusion.35 = (f32[64,1024]{1,0:T(8,128)S(1)}, f32[64,1024]{1,0:T(8,128)S(1)}) fusion(f32[64,1024]{1,0:T(8,128)S(1)} %multiply_reduce_fusion.2, f32[1024]{0:T(1024)} %param.22, f32[1024]{0:T(1024)} %param.25, bf16[256,1024]{1,0:T(8,128)(2,1)} %param.24, f32[64,288]{1,0:T(8,128)} %bitcast.35, f32[64]{0:T(128)S(1)} %add_rsqrt_fusion.1), kind=kOutput, calls=%fused_computation.69 | convolution fusion | flops 34635776 | bytes 1384704 | tf_op jit(solution)/shard_map/dot_general | solution.py:263
  18.5 0.0 copy-done.11
  18.5 0.0 copy-done.6
  18.5 0.0 copy-start.1
  18.6 0.0 copy-start.5
  18.6 0.0 copy-start.7
  18.6 0.0 copy-start.8
  18.6 5.2 %fusion.7 = (f32[64,16,1024]{2,1,0:T(8,128)}, f32[64,1024]{1,0:T(8,128)S(1)}) fusion(f32[64,16,1024]{2,1,0:T(8,128)} %param.28, f32[64,16]{1,0:T(8,128)S(1)} %get-tuple-element.10, f32[64,1024]{1,0:T(8,128)S(1)} %get-tuple-element.8, f32[16,1024]{1,0:T(8,128)S(1)} %copy-done.6, f32[64,1024]{1,0:T(8,128)S(1)} %get-tuple-element.7, ...), kind=kLoop, calls=%fused_computation.11 | loop fusion | flops 7274496 | bytes 9248832 | tf_op jit(solution)/shard_map/jit(_where)/select_n | solution.py:276
  23.8 0.9 copy-done.1
  24.7 0.0 copy-done.5
  24.7 0.0 copy-done.7
  24.7 0.0 copy-done.8
  24.7 0.0 copy-start.10
  24.7 2.5 %convolution_convert_fusion.1.x_ref = bf16[64,4096]{1,0:T(8,128)(2,1)} fusion(bf16[1024,4096]{1,0:T(8,128)(2,1)S(1)} %copy-done.1, f32[64,1024]{1,0:T(8,128)S(1)} %get-tuple-element.6, bf16[64,1024]{1,0:T(8,128)(2,1)S(1)} %copy-done.5, f32[64]{0:T(128)S(1)} %convert_element_type.60, f32[1024]{0:T(1024)S(1)} %copy-done.8, ...), kind=kOutput, calls=%fused_computation.8 | convolution fusion | flops 538247168 | bytes 9576704 | tf_op jit(solution)/shard_map/dot_general | solution.py:298
  27.2 27.6 %shard_map.194 = bf16[64,4096]{1,0:T(8,128)(2,1)} custom-call(bf16[64,4096]{1,0:T(8,128)(2,1)} %convolution_convert_fusion.1.x_ref, bf16[64,512]{1,0:T(8,128)(2,1)} %add_ref.1), custom_call_target="tpu_custom_call" | custom-call | tf_op jit(solution)/shard_map/pallas_call | solution.py:131
  54.8 1.2 multiply_reduce_fusion.1
  56.1 0.0 copy-done.10
  56.1 0.1 copy.71
  56.2 0.1 eq.34
  56.4 0.1 fusion.29
  56.5 0.2 reduce_window_sum.11
  56.6 0.2 select_reduce_fusion
  56.8 0.1 reshape.92
  56.9 0.1 copy.72
  57.0 0.1 convert_reduce_fusion
  57.2 2.7 %convolution_convert_fusion = bf16[160,4096]{1,0:T(8,128)(2,1)} fusion(f32[64]{0:T(128)S(1)} %add_rsqrt_fusion, bf16[64,4096]{1,0:T(8,128)(2,1)} %shard_map.194, bf16[160,64]{0,1:T(8,128)(2,1)S(1)} %convert_reduce_fusion), kind=kOutput, calls=%fused_computation.7 | convolution fusion | flops 85327872 | bytes 1855744 | tf_op jit(solution)/shard_map/dot_general | solution.py:307
  59.8 20.5 %shard_map.195 = bf16[4,40,4096]{2,1,0:T(8,128)(2,1)} custom-call(bf16[4,40,4096]{2,1,0:T(8,128)(2,1)} %bitcast.31), custom_call_target="tpu_custom_call" | custom-call | tf_op jit(solution)/shard_map/pallas_call | solution.py:164
  80.3 0.0 copy-start.2
  80.3 0.0 copy-start.9
  80.3 16.2 %fusion.4.x_ref = bf16[160,4096]{1,0:T(8,128)(2,1)} fusion(bf16[1,1792,4096]{2,1,0:T(8,128)(2,1)} %param.35, bf16[160,4096]{1,0:T(8,128)(2,1)} %bitcast.32, bf16[1,4096,1792]{2,1,0:T(8,128)(2,1)} %param.34), kind=kOutput, calls=%fused_computation.6 | convolution fusion | flops 4699709440 | bytes 31981568 | tf_op jit(solution)/shard_map/dot_general | solution.py:315
  96.5 37.9 %shard_map.196 = bf16[4,40,512]{2,1,0:T(8,128)(2,1)} custom-call(bf16[160,4096]{1,0:T(8,128)(2,1)} %fusion.4.x_ref), custom_call_target="tpu_custom_call" | custom-call | tf_op jit(solution)/shard_map/pallas_call | solution.py:211
  134.5 0.1 copy.73
  134.6 0.1 reshape.98
  134.8 1.8 %gather_fusion = bf16[128,512]{1,0:T(8,128)(2,1)S(1)} fusion(bf16[160,512]{1,0:T(8,128)(2,1)} %bitcast.30, s32[1024]{0:T(1024)S(1)} %pad_clamp_fusion), kind=kCustom, calls=%fused_computation | custom fusion | bytes 262656 | tf_op jit(solution)/shard_map/gather | solution.py:317
  136.6 0.2 reshape.112
  136.7 0.0 copy-done.2
  136.8 0.0 copy-done.9
  136.8 0.2 fusion.37
  137.0 0.1 copy.68
  137.1 0.1 reshape.104
  137.3 0.0 copy-start.3
  137.3 0.0 copy-start.4
  137.3 1.5 %gather_fusion.1 = f32[128]{0:T(128)S(1)} fusion(f32[64,4]{0,1:T(4,128)S(1)} %fusion.37, s32[128]{0:T(128)S(1)} %reshape.104), kind=kCustom, calls=%fused_computation.1 | custom fusion | bytes 2048 | tf_op jit(solution)/shard_map/jit(take_along_axis)/gather | solution.py:318
  138.8 0.1 reshape.107
  139.0 0.1 copy.69
  139.1 0.1 copy.70
  139.2 0.4 multiply_reduce_fusion.3
  139.6 0.1 convert_element_type.63
  139.7 0.7 add_convert_fusion
  140.3 0.0 copy-done.3
  140.3 0.0 copy-done.4
  140.3 0.9 fusion.16
  (10 shorter events, 0.1 us)
Async XLA Ops:
  0.6 1.3 copy-start
  0.6 17.9 %copy-start.6 = (f32[16,1024]{1,0:T(8,128)S(1)}, f32[16,1024]{1,0:T(8,128)}, u32[]{:S(2)}) copy-start(f32[16,1024]{1,0:T(8,128)} %param.26) | copy-start | bytes 196612
  0.7 17.9 %copy-start.11 = (s32[64]{0:T(128)S(1)}, s32[64]{0:T(128)}, u32[]{:S(2)}) copy-start(s32[64]{0:T(128)} %param.33) | copy-start | bytes 772
  18.5 6.2 %copy-start.1 = (bf16[1024,4096]{1,0:T(8,128)(2,1)S(1)}, bf16[1024,4096]{1,0:T(8,128)(2,1)}, u32[]{:S(2)}) copy-start(bf16[1024,4096]{1,0:T(8,128)(2,1)} %param.29) | copy-start | bytes 25165828
  18.6 6.2 %copy-start.5 = (bf16[64,1024]{1,0:T(8,128)(2,1)S(1)}, bf16[64,1024]{1,0:T(8,128)(2,1)}, u32[]{:S(2)}) copy-start(bf16[64,1024]{1,0:T(8,128)(2,1)} %param.19) | copy-start | bytes 393220
  18.6 6.1 %copy-start.7 = (f32[1024]{0:T(1024)S(1)}, f32[1024]{0:T(1024)}, u32[]{:S(2)}) copy-start(f32[1024]{0:T(1024)} %param.22) | copy-start | bytes 12292
  18.6 6.1 %copy-start.8 = (f32[1024]{0:T(1024)S(1)}, f32[1024]{0:T(1024)}, u32[]{:S(2)}) copy-start(f32[1024]{0:T(1024)} %param.27) | copy-start | bytes 12292
  24.7 31.4 %copy-start.10 = (s32[64,2]{0,1:T(2,128)S(1)}, s32[64,2]{0,1:T(2,128)}, u32[]{:S(2)}) copy-start(s32[64,2]{0,1:T(2,128)} %param.32) | copy-start | bytes 1540
  80.3 56.4 %copy-start.2 = (bf16[64,4096]{1,0:T(8,128)(2,1)S(1)}, bf16[64,4096]{1,0:T(8,128)(2,1)}, u32[]{:S(2)}) copy-start(bf16[64,4096]{1,0:T(8,128)(2,1)} %shard_map.194) | copy-start | bytes 1572868
  80.3 56.4 %copy-start.9 = (bf16[4096,4]{0,1:T(4,128)(2,1)S(1)}, bf16[4096,4]{0,1:T(4,128)(2,1)}, u32[]{:S(2)}) copy-start(bf16[4096,4]{0,1:T(4,128)(2,1)} %param.31) | copy-start | bytes 98308
  137.3 3.0 %copy-start.3 = (bf16[64,3,1024]{2,0,1:T(8,128)(2,1)S(1)}, bf16[64,3,1024]{2,0,1:T(8,128)(2,1)}, u32[]{:S(2)}) copy-start(bf16[64,3,1024]{2,0,1:T(8,128)(2,1)} %param.20) | copy-start | bytes 1179652
  137.3 3.0 %copy-start.4 = (bf16[64,1024]{1,0:T(8,128)(2,1)S(1)}, bf16[64,1024]{1,0:T(8,128)(2,1)}, u32[]{:S(2)}) copy-start(bf16[64,1024]{1,0:T(8,128)(2,1)} %param.18) | copy-start | bytes 393220

commit v2 on v1

--- a/solution.py
+++ b/solution.py
@@ -95,49 +95,139 @@
     return out.reshape(rows, width)
 
 
-def sum_columns_kernel(size, x_ref, add_ref, out_ref, landed, total, send_a, recv_a, send_b, recv_b):
+def split(size):
+    inner = 2 ** ((size.bit_length() - 1) // 2)
+    return (size // inner, inner) if size % inner == 0 else (size, 1)
+
+
+def remote(source, target, send_sem, recv_sem, peer):
+    copy = pltpu.make_async_remote_copy(
+        src_ref=source,
+        dst_ref=target,
+        send_sem=send_sem,
+        recv_sem=recv_sem,
+        device_id={"tensor": peer},
+        device_id_type=pl.DeviceIdType.MESH,
+    )
+    copy.start()
+    return copy
+
+
+def reduce_scatter(size, produce, own, part, near, mid, far, sems):
+    outer, inner = split(size)
     me = lax.axis_index("tensor")
+    high, low = me // inner, lax.rem(me, inner)
+    near_send, near_recv, far_send, far_recv = sems
+    copies = {}
+    hops = []
+
+    def pass_on(k):
+        for j in range(1, inner):
+            copies[k, j].wait_recv()
+            own[k] += near[k, j - 1].astype(jnp.float32)
+        if k:
+            mid[k - 1] = own[k].astype(mid.dtype)
+            peer = lax.rem(high + k, outer) * inner + low
+            hops.append(
+                remote(mid.at[k - 1], far.at[k - 1], far_send.at[k - 1], far_recv.at[k - 1], peer)
+            )
+
+    order = list(range(1, outer)) + [0]
+    for place, k in enumerate(order):
+        row = lax.rem(high + k, outer) * inner
+        for j in range(1, inner):
+            side = lax.rem(low + j, inner)
+            part[k, j - 1] = produce(row + side).astype(part.dtype)
+            copies[k, j] = remote(
+                part.at[k, j - 1],
+                near.at[k, j - 1],
+                near_send.at[k, j - 1],
+                near_recv.at[k, j - 1],
+                high * inner + side,
+            )
+        own[k] = produce(row + low)
+        if place:
+            pass_on(order[place - 1])
+    pass_on(0)
+    for k, hop in enumerate(hops):
+        hop.wait_recv()
+        own[0] += far[k].astype(jnp.float32)
+    return list(copies.values()) + hops
+
+
+def reduce_scratch(size, rows, width, kind):
+    outer, inner = split(size)
+    return [
+        pltpu.VMEM((outer, rows, width), jnp.float32),
+        pltpu.VMEM((outer, inner - 1, rows, width), kind),
+        pltpu.VMEM((outer, inner - 1, rows, width), kind),
+        pltpu.VMEM((outer - 1, rows, width), kind),
+        pltpu.VMEM((outer - 1, rows, width), kind),
+    ] + [pltpu.SemaphoreType.DMA((outer, inner - 1))] * 2 + [
+        pltpu.SemaphoreType.DMA((outer - 1,))
+    ] * 2
+
+
+def sum_columns_kernel(
+    size, x_ref, add_ref, out_ref, own, part, near, mid, far, s0, s1, s2, s3, g0, g1, g2, g3
+):
+    outer, inner = split(size)
+    me = lax.axis_index("tensor")
+    high, low = me // inner, lax.rem(me, inner)
     width = add_ref.shape[1]
     greet((("tensor", size),))
-    copies = send_all(
-        "tensor",
+    sent = reduce_scatter(
         size,
-        lambda peer, k: columns(x_ref, peer, width),
-        lambda mine, k: landed.at[k - 1],
-        send_a,
-        recv_a,
-    )
-    total[...] = add_ref[...].astype(jnp.float32) + columns(x_ref, me, width)[...].astype(jnp.float32)
-    for k, copy in enumerate(copies):
-        copy.wait_recv()
-        total[...] += landed[k].astype(jnp.float32)
-    columns(out_ref, me, width)[...] = total[...].astype(out_ref.dtype)
-    back = send_all(
-        "tensor",
-        size,
-        lambda peer, k: columns(out_ref, me, width),
-        lambda mine, k: columns(out_ref, mine, width),
-        send_b,
-        recv_b,
-    )
-    for copy in copies:
+        lambda t: columns(x_ref, t, width)[...].astype(jnp.float32),
+        own,
+        part,
+        near,
+        mid,
+        far,
+        (s0, s1, s2, s3),
+    )
+    total = own[0] + add_ref[...].astype(jnp.float32)
+    columns(out_ref, me, width)[...] = total.astype(out_ref.dtype)
+    block = columns(out_ref, me, width)
+    hops = [
+        remote(block, block, g0.at[k - 1], g1.at[k - 1], lax.rem(high + k, outer) * inner + low)
+        for k in range(1, outer)
+    ]
+
+    def spread(k):
+        block = columns(out_ref, lax.rem(high + outer - k, outer) * inner + low, width)
+        return [
+            remote(
+                block,
+                block,
+                g2.at[k, j - 1],
+                g3.at[k, j - 1],
+                high * inner + lax.rem(low + j, inner),
+            )
+            for j in range(1, inner)
+        ]
+
+    sides = spread(0)
+    for k, hop in enumerate(hops):
+        hop.wait_recv()
+        sides += spread(k + 1)
+    for copy in sent + hops:
         copy.wait_send()
-    for copy in back:
+    for copy in sides:
         copy.wait()
 
 
 def sum_columns(x, add, size, collective_id):
     rows, width = add.shape
+    outer, inner = split(size)
     return pl.pallas_call(
         functools.partial(sum_columns_kernel, size),
         out_shape=jax.ShapeDtypeStruct(x.shape, x.dtype),
         in_specs=[VMEM] * 2,
         out_specs=VMEM,
-        scratch_shapes=[
-            pltpu.VMEM((size - 1, rows, width), x.dtype),
-            pltpu.VMEM((rows, width), jnp.float32),
-        ]
-        + [pltpu.SemaphoreType.DMA((size - 1,))] * 4,
+        scratch_shapes=reduce_scratch(size, rows, width, x.dtype)
+        + [pltpu.SemaphoreType.DMA((outer - 1,))] * 2
+        + [pltpu.SemaphoreType.DMA((outer, inner - 1))] * 2,
         compiler_params=pltpu.CompilerParams(collective_id=collective_id, has_side_effects=True),
     )(x, add)
 
@@ -171,57 +261,68 @@
     )(x)
 
 
-def combine_kernel(size, groups, x_ref, out_ref, landed, total, reply, send_a, recv_a, send_b, recv_b):
+def combine_kernel(
+    size, groups, x_ref, w_ref, out_ref, weights, load, reply, b0, b1,
+    own, part, near, mid, far, s0, s1, s2, s3
+):
+    outer, inner = split(size)
     me = lax.axis_index("tensor")
+    high, low = me // inner, lax.rem(me, inner)
     home = lax.axis_index("dp")
-    width = total.shape[1]
-    rows = reply.shape[1]
+    rows, width = reply.shape[1:]
+    loads = []
+    for k in list(range(1, outer)) + [0]:
+        for j in list(range(1, inner)) + [0]:
+            t = lax.rem(high + k, outer) * inner + lax.rem(low + j, inner)
+            place = len(loads)
+            loads.append(
+                pltpu.make_async_copy(columns(w_ref, t, width), weights.at[place], load.at[place])
+            )
+            loads[-1].start()
     greet((("tensor", size), ("dp", groups)))
-    copies = send_all(
-        "tensor",
-        size,
-        lambda peer, k: columns(x_ref, peer, width),
-        lambda mine, k: landed.at[k - 1],
-        send_a,
-        recv_a,
-    )
-    total[...] = columns(x_ref, me, width)[...].astype(jnp.float32)
-    for k, copy in enumerate(copies):
-        copy.wait_recv()
-        total[...] += landed[k].astype(jnp.float32)
+    turn = iter(range(size))
+
+    def produce(t):
+        place = next(turn)
+        loads[place].wait()
+        return jnp.dot(x_ref[...], weights[place], preferred_element_type=jnp.float32).astype(
+            x_ref.dtype
+        ).astype(jnp.float32)
+
+    sent = reduce_scatter(size, produce, own, part, near, mid, far, (s0, s1, s2, s3))
     for block in range(groups):
-        reply[block] = total[block * rows : (block + 1) * rows, :].astype(reply.dtype)
+        reply[block] = own[0, block * rows : (block + 1) * rows, :].astype(reply.dtype)
     back = send_all(
         "dp",
         groups,
         lambda peer, k: reply.at[peer],
         lambda mine, k: out_ref.at[mine],
-        send_b,
-        recv_b,
+        b0,
+        b1,
     )
     out_ref[home] = reply[home]
-    for copy in copies:
+    for copy in sent:
         copy.wait_send()
     for copy in back:
         copy.wait()
 
 
-def combine(x, size, groups, collective_id):
-    rows, width = x.shape[0] // groups, x.shape[1] // size
+def combine(x, w, size, groups, collective_id):
+    rows, width = x.shape[0] // groups, w.shape[1] // size
     return pl.pallas_call(
         functools.partial(combine_kernel, size, groups),
         out_shape=jax.ShapeDtypeStruct((groups, rows, width), x.dtype),
-        in_specs=[VMEM],
+        in_specs=[VMEM, pl.BlockSpec(memory_space=pl.ANY)],
         out_specs=VMEM,
         scratch_shapes=[
-            pltpu.VMEM((size - 1, x.shape[0], width), x.dtype),
-            pltpu.VMEM((x.shape[0], width), jnp.float32),
+            pltpu.VMEM((size, w.shape[0], width), w.dtype),
+            pltpu.SemaphoreType.DMA((size,)),
             pltpu.VMEM((groups, rows, width), x.dtype),
         ]
-        + [pltpu.SemaphoreType.DMA((size - 1,))] * 2
-        + [pltpu.SemaphoreType.DMA((groups - 1,))] * 2,
+        + [pltpu.SemaphoreType.DMA((groups - 1,))] * 2
+        + reduce_scratch(size, x.shape[0], width, x.dtype),
         compiler_params=pltpu.CompilerParams(collective_id=collective_id, has_side_effects=True),
-    )(x)
+    )(x, w)
 
 
 def local(
@@ -312,8 +413,7 @@
     )
     hidden = jax.nn.silu(up_sum).astype(jnp.bfloat16)
     down_rows = down_weight[0]
-    expert_part = jnp.dot(hidden, down_rows, preferred_element_type=jnp.float32)
-    returned = combine(expert_part.astype(jnp.bfloat16), n_tensor, n_dp, 3)
+    returned = combine(hidden, down_rows, n_tensor, n_dp, 3)
     gathered = returned.reshape(-1, slice_width)[buffer_row]
     chosen_logit = jnp.take_along_axis(raw_logits, expert_ids, axis=1) * inv_rms[:, None]
     first = 1.0 / (1.0 + jnp.exp(chosen_logit[:, 1] - chosen_logit[:, 0]))

time: 142 us -> 127 us (0.89)
  Pallas kernels: 97.6 us -> 88.9 us
  matrix products: 24.8 us -> 17.6 us
    dot_general x1, matrix products: 16.2 us -> 9.03 us  [local(): jnp.dot(incoming.reshape(-1, incoming.shape[2]), up_rows, preferred_eleme...]
    pallas_call x1, Pallas kernels: 37.9 us -> 31.6 us  [combine(): pl.pallas_call(functools.partial(combine_kernel, size, groups), out_shape...]
    pallas_call x1, Pallas kernels: 27.6 us -> 21.8 us  [sum_columns(): pl.pallas_call(functools.partial(sum_columns_kernel, size), out_shape=jax...]
    pallas_call x1, Pallas kernels: 20.5 us -> 24 us  [dispatch(): pl.pallas_call(functools.partial(dispatch_kernel, size), out_shape=jax.Sh...]
where the time goes in v2:
time: 127 us; the launch traced here: 125 us
  Pallas kernels  88.9 us (70%)
  matrix products  17.6 us (14%)
  other arithmetic  11.2 us (9%)
  local copies, waits for them, and re-layouts  6.6 us (5%)
    pallas_call x1, Pallas kernels, combine(): pl.pallas_call(functools.partial(combine_kernel, size, groups), out_shape...  31.6 us
    pallas_call x1, Pallas kernels, dispatch(): pl.pallas_call(functools.partial(dispatch_kernel, size), out_shape=jax.Sh...  24 us
    pallas_call x1, Pallas kernels, sum_columns(): pl.pallas_call(functools.partial(sum_columns_kernel, size), out_shape=jax...  21.8 us
    pallas_call x1, Pallas kernels, sum_rows(): pl.pallas_call(functools.partial(sum_rows_kernel, size), out_shape=jax.Sh...  11.6 us
    dot_general x1, matrix products, local(): jnp.dot(incoming.reshape(-1, incoming.shape[2]), up_rows, preferred_eleme...  9.03 us
    select_n x1, other arithmetic, local(): state_out = jnp.where(live_mask[:, None, None], state_next, scan_state)  5.23 us
    dot_general x1, matrix products, local(): jnp.dot(placement, normed, preferred_element_type=jnp.float32)  2.68 us

profile of v2, /device:TPU:11, one launch (start us, length us, event | category | flops | bytes accessed | tf_op | source)
XLA Modules:
  0.0 125.2 jit_solution(5192597229967742397)
XLA Ops:
  0.6 0.0 copy-start
  0.6 0.0 copy-start.6
  0.7 0.0 copy-start.11
  0.7 1.2 multiply_reduce_fusion.2
  1.9 0.0 copy-done
  1.9 1.7 %convolution_bitcast_fusion.x_ref = f32[8,8,288]{2,1,0:T(8,128)} fusion(bf16[1024,288]{0,1:T(8,128)(2,1)S(1)} %copy-done, f32[64,1024]{1,0:T(8,128)S(1)} %multiply_reduce_fusion.2, f32[1024]{0:T(1024)} %param.22), kind=kOutput, calls=%fused_computation.11 | convolution fusion | flops 38141952 | bytes 929792 | tf_op jit(solution)/shard_map/dot_general | solution.py:353
  3.6 11.6 %shard_map.193 = f32[8,8,288]{2,1,0:T(8,128)} custom-call(f32[8,8,288]{2,1,0:T(8,128)} %convolution_bitcast_fusion.x_ref), custom_call_target="tpu_custom_call" | custom-call | tf_op jit(solution)/shard_map/pallas_call | solution.py:86
  15.2 0.9 fusion.27
  16.1 0.9 multiply_reduce_fusion.4
  17.1 1.5 %fusion.26 = (f32[64,1024]{1,0:T(8,128)S(1)}, f32[64,1024]{1,0:T(8,128)S(1)}) fusion(f32[64,1024]{1,0:T(8,128)S(1)} %multiply_reduce_fusion.2, f32[1024]{0:T(1024)} %param.22, f32[1024]{0:T(1024)} %param.25, bf16[256,1024]{1,0:T(8,128)(2,1)} %param.24, f32[64,288]{1,0:T(8,128)} %bitcast.30, f32[64]{0:T(128)S(1)} %add_rsqrt_fusion.1), kind=kOutput, calls=%fused_computation.64 | convolution fusion | flops 34635776 | bytes 1384704 | tf_op jit(solution)/shard_map/dot_general | solution.py:364
  18.5 0.0 copy-done.11
  18.5 0.0 copy-done.6
  18.5 0.0 copy-start.1
  18.6 0.0 copy-start.5
  18.6 0.0 copy-start.7
  18.6 0.0 copy-start.8
  18.6 5.2 %fusion.2 = (f32[64,16,1024]{2,1,0:T(8,128)}, f32[64,1024]{1,0:T(8,128)S(1)}) fusion(f32[64,16,1024]{2,1,0:T(8,128)} %param.28, f32[64,16]{1,0:T(8,128)S(1)} %get-tuple-element.10, f32[64,1024]{1,0:T(8,128)S(1)} %get-tuple-element.8, f32[16,1024]{1,0:T(8,128)S(1)} %copy-done.6, f32[64,1024]{1,0:T(8,128)S(1)} %get-tuple-element.7, ...), kind=kLoop, calls=%fused_computation.8 | loop fusion | flops 7274496 | bytes 9248832 | tf_op jit(solution)/shard_map/jit(_where)/select_n | solution.py:377
  23.8 0.9 copy-done.1
  24.7 0.0 copy-done.5
  24.7 0.0 copy-done.7
  24.7 0.0 copy-done.8
  24.7 0.0 copy-start.10
  24.7 2.5 %convolution_convert_fusion.1.x_ref = bf16[64,4096]{1,0:T(8,128)(2,1)} fusion(bf16[1024,4096]{1,0:T(8,128)(2,1)S(1)} %copy-done.1, f32[64,1024]{1,0:T(8,128)S(1)} %get-tuple-element.6, bf16[64,1024]{1,0:T(8,128)(2,1)S(1)} %copy-done.5, f32[64]{0:T(128)S(1)} %convert_element_type.57, f32[1024]{0:T(1024)S(1)} %copy-done.8, ...), kind=kOutput, calls=%fused_computation.5 | convolution fusion | flops 538247168 | bytes 9576704 | tf_op jit(solution)/shard_map/dot_general | solution.py:399
  27.2 21.8 %shard_map.194 = bf16[64,4096]{1,0:T(8,128)(2,1)} custom-call(bf16[64,4096]{1,0:T(8,128)(2,1)} %convolution_convert_fusion.1.x_ref, bf16[64,512]{1,0:T(8,128)(2,1)} %add_ref.1), custom_call_target="tpu_custom_call" | custom-call | tf_op jit(solution)/shard_map/pallas_call | solution.py:223
  49.0 1.2 multiply_reduce_fusion.1
  50.3 0.0 copy-done.10
  50.3 0.1 copy.71
  50.4 0.1 eq.34
  50.5 0.1 fusion.21
  50.6 0.2 reduce_window_sum.11
  50.8 0.2 select_reduce_fusion
  51.0 0.1 reshape.92
  51.1 0.1 copy.72
  51.2 0.1 convert_reduce_fusion
  51.3 2.7 %convolution_convert_fusion = bf16[160,4096]{1,0:T(8,128)(2,1)} fusion(f32[64]{0:T(128)S(1)} %add_rsqrt_fusion, bf16[64,4096]{1,0:T(8,128)(2,1)} %shard_map.194, bf16[160,64]{0,1:T(8,128)(2,1)S(1)} %convert_reduce_fusion), kind=kOutput, calls=%fused_computation.4 | convolution fusion | flops 85327872 | bytes 1855744 | tf_op jit(solution)/shard_map/dot_general | solution.py:408
  54.0 24.0 %shard_map.195 = bf16[4,40,4096]{2,1,0:T(8,128)(2,1)} custom-call(bf16[4,40,4096]{2,1,0:T(8,128)(2,1)} %bitcast.26), custom_call_target="tpu_custom_call" | custom-call | tf_op jit(solution)/shard_map/pallas_call | solution.py:254
  78.0 9.0 %multiply_convert_fusion.x_ref = bf16[160,1792]{1,0:T(8,128)(2,1)} fusion(bf16[160,4096]{1,0:T(8,128)(2,1)} %bitcast.27, bf16[1,4096,1792]{2,1,0:T(8,128)(2,1)} %param.34), kind=kOutput, calls=%fused_computation.10 | convolution fusion | flops 2350243840 | bytes 16564224 | tf_op jit(solution)/shard_map/dot_general | solution.py:411
  87.0 0.0 copy-start.2
  87.0 0.0 copy-start.9
  87.0 31.6 %shard_map.196 = bf16[4,40,512]{2,1,0:T(8,128)(2,1)} custom-call(bf16[160,1792]{1,0:T(8,128)(2,1)} %multiply_convert_fusion.x_ref, bf16[1792,4096]{1,0:T(8,128)(2,1)} %bitcast.24), custom_call_target="tpu_custom_call" | custom-call | tf_op jit(solution)/shard_map/pallas_call | solution.py:312
  118.6 0.1 copy.73
  118.7 0.1 reshape.98
  118.8 1.8 %gather_fusion = bf16[128,512]{1,0:T(8,128)(2,1)S(1)} fusion(bf16[160,512]{1,0:T(8,128)(2,1)} %bitcast.25, s32[1024]{0:T(1024)S(1)} %pad_clamp_fusion), kind=kCustom, calls=%fused_computation | custom fusion | bytes 262656 | tf_op jit(solution)/shard_map/gather | solution.py:417
  120.6 0.2 reshape.112
  120.8 0.0 copy-done.2
  120.8 0.0 copy-done.9
  120.8 0.2 fusion.28
  121.1 0.1 copy.68
  121.2 0.1 reshape.104
  121.4 0.0 copy-start.3
  121.4 0.0 copy-start.4
  121.4 1.5 %gather_fusion.1 = f32[128]{0:T(128)S(1)} fusion(f32[64,4]{0,1:T(4,128)S(1)} %fusion.28, s32[128]{0:T(128)S(1)} %reshape.104), kind=kCustom, calls=%fused_computation.1 | custom fusion | bytes 2048 | tf_op jit(solution)/shard_map/jit(take_along_axis)/gather | solution.py:418
  122.9 0.1 reshape.107
  123.0 0.1 copy.69
  123.2 0.1 copy.70
  123.3 0.4 multiply_reduce_fusion.3
  123.7 0.1 convert_element_type.60
  123.7 0.7 add_convert_fusion
  124.4 0.0 copy-done.3
  124.4 0.0 copy-done.4
  124.4 0.9 fusion.8
  (10 shorter events, 0.1 us)
Async XLA Ops:
  0.6 1.3 %copy-start = (bf16[1024,288]{0,1:T(8,128)(2,1)S(1)}, bf16[1024,288]{0,1:T(8,128)(2,1)}, u32[]{:S(2)}) copy-start(bf16[1024,288]{0,1:T(8,128)(2,1)} %param.23) | copy-start | bytes 1769476
  0.6 17.9 %copy-start.6 = (f32[16,1024]{1,0:T(8,128)S(1)}, f32[16,1024]{1,0:T(8,128)}, u32[]{:S(2)}) copy-start(f32[16,1024]{1,0:T(8,128)} %param.26) | copy-start | bytes 196612
  0.7 17.9 %copy-start.11 = (s32[64]{0:T(128)S(1)}, s32[64]{0:T(128)}, u32[]{:S(2)}) copy-start(s32[64]{0:T(128)} %param.33) | copy-start | bytes 772
  18.5 6.2 %copy-start.1 = (bf16[1024,4096]{1,0:T(8,128)(2,1)S(1)}, bf16[1024,4096]{1,0:T(8,128)(2,1)}, u32[]{:S(2)}) copy-start(bf16[1024,4096]{1,0:T(8,128)(2,1)} %param.29) | copy-start | bytes 25165828
  18.6 6.2 %copy-start.5 = (bf16[64,1024]{1,0:T(8,128)(2,1)S(1)}, bf16[64,1024]{1,0:T(8,128)(2,1)}, u32[]{:S(2)}) copy-start(bf16[64,1024]{1,0:T(8,128)(2,1)} %param.19) | copy-start | bytes 393220
  18.6 6.1 %copy-start.7 = (f32[1024]{0:T(1024)S(1)}, f32[1024]{0:T(1024)}, u32[]{:S(2)}) copy-start(f32[1024]{0:T(1024)} %param.22) | copy-start | bytes 12292
  18.6 6.1 %copy-start.8 = (f32[1024]{0:T(1024)S(1)}, f32[1024]{0:T(1024)}, u32[]{:S(2)}) copy-start(f32[1024]{0:T(1024)} %param.27) | copy-start | bytes 12292
  24.7 25.6 %copy-start.10 = (s32[64,2]{0,1:T(2,128)S(1)}, s32[64,2]{0,1:T(2,128)}, u32[]{:S(2)}) copy-start(s32[64,2]{0,1:T(2,128)} %param.32) | copy-start | bytes 1540
  87.0 33.8 %copy-start.2 = (bf16[64,4096]{1,0:T(8,128)(2,1)S(1)}, bf16[64,4096]{1,0:T(8,128)(2,1)}, u32[]{:S(2)}) copy-start(bf16[64,4096]{1,0:T(8,128)(2,1)} %shard_map.194) | copy-start | bytes 1572868
  87.0 33.8 %copy-start.9 = (bf16[4096,4]{0,1:T(4,128)(2,1)S(1)}, bf16[4096,4]{0,1:T(4,128)(2,1)}, u32[]{:S(2)}) copy-start(bf16[4096,4]{0,1:T(4,128)(2,1)} %param.31) | copy-start | bytes 98308
  121.4 3.0 %copy-start.3 = (bf16[64,3,1024]{2,0,1:T(8,128)(2,1)S(1)}, bf16[64,3,1024]{2,0,1:T(8,128)(2,1)}, u32[]{:S(2)}) copy-start(bf16[64,3,1024]{2,0,1:T(8,128)(2,1)} %param.20) | copy-start | bytes 1179652
  121.4 3.0 %copy-start.4 = (bf16[64,1024]{1,0:T(8,128)(2,1)S(1)}, bf16[64,1024]{1,0:T(8,128)(2,1)}, u32[]{:S(2)}) copy-start(bf16[64,1024]{1,0:T(8,128)(2,1)} %param.18) | copy-start | bytes 393220

commit v3 on v2

--- a/solution.py
+++ b/solution.py
@@ -414,14 +414,22 @@
     hidden = jax.nn.silu(up_sum).astype(jnp.bfloat16)
     down_rows = down_weight[0]
     returned = combine(hidden, down_rows, n_tensor, n_dp, 3)
-    gathered = returned.reshape(-1, slice_width)[buffer_row]
-    chosen_logit = jnp.take_along_axis(raw_logits, expert_ids, axis=1) * inv_rms[:, None]
+    chosen = expert_ids[:, :, None] == jnp.arange(experts_total, dtype=jnp.int32)
+    chosen_logit = (
+        jnp.sum(jnp.where(chosen, raw_logits[:, None, :], 0.0), axis=2) * inv_rms[:, None]
+    )
     first = 1.0 / (1.0 + jnp.exp(chosen_logit[:, 1] - chosen_logit[:, 0]))
     second = 1.0 / (1.0 + jnp.exp(chosen_logit[:, 0] - chosen_logit[:, 1]))
     route_weight = jnp.stack([first, second], axis=1) * live_float[:, None]
-    layer_out = (
-        hidden_local + jnp.sum(route_weight[:, :, None] * gathered.astype(jnp.float32), axis=1)
-    ).astype(jnp.bfloat16)
+    mix = jnp.sum(
+        jnp.where(buffer_row[:, :, None] == row_numbers, route_weight[:, :, None], 0.0), axis=1
+    )
+    expert_sum = jnp.dot(
+        mix,
+        returned.reshape(-1, slice_width).astype(jnp.float32),
+        precision=lax.Precision.HIGHEST,
+    )
+    layer_out = (hidden_local + expert_sum).astype(jnp.bfloat16)
     return (layer_out, state_out, conv_cache)
 
 

time: 127 us -> 123 us (0.969)
  local copies, waits for them, and re-layouts: 6.6 us -> 2.3 us
  matrix products: 17.6 us -> 19.4 us
    gather x6 -> x0, local copies, waits for them, and re-layouts: 3.76 us -> none  [the longest x5 1.95 us: local(): jnp.take_along_axis(raw_logits, expert_ids, axis=1) * inv_rms[:, None]]
    dot_general x0 -> x1, matrix products: none -> 1.77 us  [local(): jnp.dot(mix, returned.reshape(-1, slice_width).astype(jnp.float32), preci...]
where the time goes in v3:
time: 123 us; the launch traced here: 122 us
  Pallas kernels  88.9 us (72%)
  matrix products  19.4 us (16%)
  other arithmetic  10.3 us (8%)
  local copies, waits for them, and re-layouts  2.3 us (2%)
    pallas_call x1, Pallas kernels, combine(): pl.pallas_call(functools.partial(combine_kernel, size, groups), out_shape...  31.6 us
    pallas_call x1, Pallas kernels, dispatch(): pl.pallas_call(functools.partial(dispatch_kernel, size), out_shape=jax.Sh...  24 us
    pallas_call x1, Pallas kernels, sum_columns(): pl.pallas_call(functools.partial(sum_columns_kernel, size), out_shape=jax...  21.8 us
    pallas_call x1, Pallas kernels, sum_rows(): pl.pallas_call(functools.partial(sum_rows_kernel, size), out_shape=jax.Sh...  11.6 us
    dot_general x1, matrix products, local(): jnp.dot(incoming.reshape(-1, incoming.shape[2]), up_rows, preferred_eleme...  9.03 us
    select_n x1, other arithmetic, local(): state_out = jnp.where(live_mask[:, None, None], state_next, scan_state)  5.23 us
    dot_general x1, matrix products, local(): jnp.dot(placement, normed, preferred_element_type=jnp.float32)  2.68 us
    dot_general x1, matrix products, local(): mixer_part = jnp.dot(gated, output_proj, preferred_element_type=jnp.float32)  2.51 us

profile of v3, /device:TPU:11, one launch (start us, length us, event | category | flops | bytes accessed | tf_op | source)
XLA Modules:
  0.0 121.8 jit_solution(12455578925957494595)
XLA Ops:
  0.6 0.0 copy-start
  0.6 0.0 copy-start.11
  0.7 0.0 copy-start.6
  0.7 1.2 %multiply_reduce_fusion.2 = f32[64,1024]{1,0:T(8,128)S(1)} fusion(bf16[64,1,1024]{2,0,1:T(8,128)(2,1)} %bitcast.29, bf16[64,3,1024]{2,0,1:T(8,128)(2,1)} %param.20, f32[4,1024]{1,0:T(4,128)} %param.21), kind=kLoop, calls=%fused_computation.14 | loop fusion | flops 983040 | bytes 802816 | tf_op jit(solution)/shard_map/reduce_sum | solution.py:351
  1.9 0.0 copy-done
  1.9 1.7 %convolution_bitcast_fusion.x_ref = f32[8,8,288]{2,1,0:T(8,128)} fusion(bf16[1024,288]{0,1:T(8,128)(2,1)S(1)} %copy-done, f32[64,1024]{1,0:T(8,128)S(1)} %multiply_reduce_fusion.2, f32[1024]{0:T(1024)} %param.22), kind=kOutput, calls=%fused_computation.11 | convolution fusion | flops 38141952 | bytes 929792 | tf_op jit(solution)/shard_map/dot_general | solution.py:353
  3.6 11.6 %shard_map.193 = f32[8,8,288]{2,1,0:T(8,128)} custom-call(f32[8,8,288]{2,1,0:T(8,128)} %convolution_bitcast_fusion.x_ref), custom_call_target="tpu_custom_call" | custom-call | tf_op jit(solution)/shard_map/pallas_call | solution.py:86
  15.2 0.9 multiply_reduce_fusion.3
  16.1 1.5 %fusion.26 = (f32[64,1024]{1,0:T(8,128)S(1)}, f32[64,1024]{1,0:T(8,128)S(1)}) fusion(f32[64,1024]{1,0:T(8,128)S(1)} %multiply_reduce_fusion.2, f32[1024]{0:T(1024)} %param.22, f32[1024]{0:T(1024)} %param.25, bf16[256,1024]{1,0:T(8,128)(2,1)} %param.24, f32[64,288]{1,0:T(8,128)} %bitcast.27, f32[64]{0:T(128)S(1)} %add_rsqrt_fusion.1), kind=kOutput, calls=%fused_computation.61 | convolution fusion | flops 34635776 | bytes 1384704 | tf_op jit(solution)/shard_map/dot_general | solution.py:364
  17.6 0.9 fusion.27
  18.5 0.0 copy-done.11
  18.5 0.0 copy-done.6
  18.5 0.0 copy-start.1
  18.5 0.0 copy-start.5
  18.5 0.0 copy-start.7
  18.6 0.0 copy-start.8
  18.6 5.2 %fusion.2 = (f32[64,16,1024]{2,1,0:T(8,128)}, f32[64,1024]{1,0:T(8,128)S(1)}) fusion(f32[64,16,1024]{2,1,0:T(8,128)} %param.28, f32[64,16]{1,0:T(8,128)S(1)} %get-tuple-element.8, f32[64,1024]{1,0:T(8,128)S(1)} %get-tuple-element.6, f32[16,1024]{1,0:T(8,128)S(1)} %copy-done.6, f32[64,1024]{1,0:T(8,128)S(1)} %get-tuple-element.5, ...), kind=kLoop, calls=%fused_computation.6 | loop fusion | flops 7274496 | bytes 9248832 | tf_op jit(solution)/shard_map/jit(_where)/select_n | solution.py:377
  23.8 0.9 copy-done.1
  24.7 0.0 copy-done.5
  24.7 0.0 copy-done.7
  24.7 0.0 copy-done.8
  24.7 0.0 copy-start.10
  24.7 2.5 %convolution_convert_fusion.1.x_ref = bf16[64,4096]{1,0:T(8,128)(2,1)} fusion(bf16[1024,4096]{1,0:T(8,128)(2,1)S(1)} %copy-done.1, f32[64,1024]{1,0:T(8,128)S(1)} %get-tuple-element.4, bf16[64,1024]{1,0:T(8,128)(2,1)S(1)} %copy-done.5, f32[64]{0:T(128)S(1)} %convert_element_type.55, f32[1024]{0:T(1024)S(1)} %copy-done.8, ...), kind=kOutput, calls=%fused_computation.3 | convolution fusion | flops 538247168 | bytes 9576704 | tf_op jit(solution)/shard_map/dot_general | solution.py:399
  27.2 21.8 %shard_map.194 = bf16[64,4096]{1,0:T(8,128)(2,1)} custom-call(bf16[64,4096]{1,0:T(8,128)(2,1)} %convolution_convert_fusion.1.x_ref, bf16[64,512]{1,0:T(8,128)(2,1)} %add_ref.1), custom_call_target="tpu_custom_call" | custom-call | tf_op jit(solution)/shard_map/pallas_call | solution.py:223
  49.0 1.2 %multiply_reduce_fusion.1 = f32[64]{0:T(128)S(1)} fusion(bf16[64,4096]{1,0:T(8,128)(2,1)} %shard_map.194), kind=kLoop, calls=%fused_computation.13 | loop fusion | flops 786368 | bytes 524544 | tf_op jit(solution)/shard_map/reduce_sum | solution.py:403
  50.2 0.0 copy-done.10
  50.3 0.1 copy.42
  50.4 0.1 eq.60
  50.5 0.1 fusion.22
  50.6 0.2 reduce_window_sum.11
  50.8 0.2 select_reduce_fusion.1
  50.9 0.1 reshape.85
  51.1 0.1 copy.43
  51.2 0.1 convert_reduce_fusion
  51.3 2.7 %convolution_convert_fusion = bf16[160,4096]{1,0:T(8,128)(2,1)} fusion(f32[64]{0:T(128)S(1)} %add_rsqrt_fusion, bf16[64,4096]{1,0:T(8,128)(2,1)} %shard_map.194, bf16[160,64]{0,1:T(8,128)(2,1)S(1)} %convert_reduce_fusion), kind=kOutput, calls=%fused_computation.2 | convolution fusion | flops 85327872 | bytes 1855744 | tf_op jit(solution)/shard_map/dot_general | solution.py:408
  54.0 24.0 %shard_map.195 = bf16[4,40,4096]{2,1,0:T(8,128)(2,1)} custom-call(bf16[4,40,4096]{2,1,0:T(8,128)(2,1)} %bitcast.23), custom_call_target="tpu_custom_call" | custom-call | tf_op jit(solution)/shard_map/pallas_call | solution.py:254
  78.0 9.0 %multiply_convert_fusion.x_ref = bf16[160,1792]{1,0:T(8,128)(2,1)} fusion(bf16[160,4096]{1,0:T(8,128)(2,1)} %bitcast.24, bf16[1,4096,1792]{2,1,0:T(8,128)(2,1)} %param.34), kind=kOutput, calls=%fused_computation.8 | convolution fusion | flops 2350243840 | bytes 16564224 | tf_op jit(solution)/shard_map/dot_general | solution.py:411
  87.0 0.0 copy-start.2
  87.0 0.0 copy-start.9
  87.0 0.0 copy-start.3
  87.0 0.0 copy-start.4
  87.0 31.6 %shard_map.196 = bf16[4,40,512]{2,1,0:T(8,128)(2,1)} custom-call(bf16[160,1792]{1,0:T(8,128)(2,1)} %multiply_convert_fusion.x_ref, bf16[1792,4096]{1,0:T(8,128)(2,1)} %bitcast.22), custom_call_target="tpu_custom_call" | custom-call | tf_op jit(solution)/shard_map/pallas_call | solution.py:312
  118.6 0.0 copy-done.2
  118.6 0.0 copy-done.9
  118.6 0.2 fusion.28
  118.9 0.1 select_reduce_fusion
  119.0 0.1 convert_element_type.58
  119.1 1.8 %fusion.5 = bf16[64,512]{1,0:T(8,128)(2,1)} fusion(f32[64,160]{1,0:T(8,128)S(1)} %select_reduce_fusion, bf16[160,512]{1,0:T(8,128)(2,1)} %bitcast.25, f32[64,4096]{1,0:T(8,128)S(1)} %convert_element_type.58, s32[]{:T(128)S(6)} %select_n.24), kind=kOutput, calls=%fused_computation.10 | convolution fusion | flops 62980096 | bytes 401412 | tf_op jit(solution)/shard_map/dot_general | solution.py:427
  120.9 0.0 copy-done.3
  120.9 0.0 copy-done.4
  120.9 0.9 fusion.9
  (9 shorter events, 0.1 us)
Async XLA Ops:
  0.6 1.3 %copy-start = (bf16[1024,288]{0,1:T(8,128)(2,1)S(1)}, bf16[1024,288]{0,1:T(8,128)(2,1)}, u32[]{:S(2)}) copy-start(bf16[1024,288]{0,1:T(8,128)(2,1)} %param.23) | copy-start | bytes 1769476
  0.6 17.9 %copy-start.11 = (s32[64]{0:T(128)S(1)}, s32[64]{0:T(128)}, u32[]{:S(2)}) copy-start(s32[64]{0:T(128)} %param.33) | copy-start | bytes 772
  0.7 17.9 %copy-start.6 = (f32[16,1024]{1,0:T(8,128)S(1)}, f32[16,1024]{1,0:T(8,128)}, u32[]{:S(2)}) copy-start(f32[16,1024]{1,0:T(8,128)} %param.26) | copy-start | bytes 196612
  18.5 6.2 %copy-start.1 = (bf16[1024,4096]{1,0:T(8,128)(2,1)S(1)}, bf16[1024,4096]{1,0:T(8,128)(2,1)}, u32[]{:S(2)}) copy-start(bf16[1024,4096]{1,0:T(8,128)(2,1)} %param.29) | copy-start | bytes 25165828
  18.5 6.2 %copy-start.5 = (bf16[64,1024]{1,0:T(8,128)(2,1)S(1)}, bf16[64,1024]{1,0:T(8,128)(2,1)}, u32[]{:S(2)}) copy-start(bf16[64,1024]{1,0:T(8,128)(2,1)} %param.19) | copy-start | bytes 393220
  18.5 6.1 %copy-start.7 = (f32[1024]{0:T(1024)S(1)}, f32[1024]{0:T(1024)}, u32[]{:S(2)}) copy-start(f32[1024]{0:T(1024)} %param.22) | copy-start | bytes 12292
  18.6 6.1 %copy-start.8 = (f32[1024]{0:T(1024)S(1)}, f32[1024]{0:T(1024)}, u32[]{:S(2)}) copy-start(f32[1024]{0:T(1024)} %param.27) | copy-start | bytes 12292
  24.7 25.6 %copy-start.10 = (s32[64,2]{0,1:T(2,128)S(1)}, s32[64,2]{0,1:T(2,128)}, u32[]{:S(2)}) copy-start(s32[64,2]{0,1:T(2,128)} %param.32) | copy-start | bytes 1540
  87.0 31.6 %copy-start.2 = (bf16[64,4096]{1,0:T(8,128)(2,1)S(1)}, bf16[64,4096]{1,0:T(8,128)(2,1)}, u32[]{:S(2)}) copy-start(bf16[64,4096]{1,0:T(8,128)(2,1)} %shard_map.194) | copy-start | bytes 1572868
  87.0 31.6 %copy-start.9 = (bf16[4096,4]{0,1:T(4,128)(2,1)S(1)}, bf16[4096,4]{0,1:T(4,128)(2,1)}, u32[]{:S(2)}) copy-start(bf16[4096,4]{0,1:T(4,128)(2,1)} %param.31) | copy-start | bytes 98308
  87.0 33.9 %copy-start.3 = (bf16[64,3,1024]{2,0,1:T(8,128)(2,1)S(1)}, bf16[64,3,1024]{2,0,1:T(8,128)(2,1)}, u32[]{:S(2)}) copy-start(bf16[64,3,1024]{2,0,1:T(8,128)(2,1)} %param.20) | copy-start | bytes 1179652
  87.0 33.9 %copy-start.4 = (bf16[64,1024]{1,0:T(8,128)(2,1)S(1)}, bf16[64,1024]{1,0:T(8,128)(2,1)}, u32[]{:S(2)}) copy-start(bf16[64,1024]{1,0:T(8,128)(2,1)} %param.18) | copy-start | bytes 393220
